TPU v7x, 32 devices: a whole 2x2x4 slice. The times are simulated.
32 devices in a mesh: dp: 2 (over x), ha: 4 (over z), wa: 4 (over y, core).
Axes of the slice: x: 2, y: 2, z: 4, core: 2. Of those that a mesh axis runs over, the one named last changes fastest.
Arguments:
- query_in: bfloat16 [2, 4, 4, 384, 512], P('dp', 'ha', 'wa'), may hold values from -30 to 30
- key_in: bfloat16 [2, 4, 4, 384, 512], P('dp', 'ha', 'wa'), may hold values from -6 to 6
- value_in: bfloat16 [2, 4, 4, 384, 512], P('dp', 'ha', 'wa'), may hold values from -6 to 6
- grad_out: bfloat16 [2, 4, 4, 384, 3072], P('dp', 'ha', 'wa'), may hold values from -1.5 to 1.5
- out_weight: bfloat16 [512, 3072], P('dp'), may hold values from -0.25 to 0.25
Outputs:
- outcome: bfloat16 [2, 4, 4, 384, 3072], P('dp', 'ha', 'wa')
- query_grad: float32 [2, 4, 4, 384, 512], P('dp', 'ha', 'wa')
- key_grad: float32 [2, 4, 4, 384, 512], P('dp', 'ha', 'wa')
- value_grad: float32 [2, 4, 4, 384, 512], P('dp', 'ha', 'wa')
- weight_grad: float32 [512, 3072], P('dp')
All inputs are finite; a program needn't handle non-finite values.
Results may differ from a plain program's by a relative error of at most 0.035.
Values may be sent and summed in bfloat16 or wider, within the bound.
No kernel may reach another device: no remote copies, remote signals or barrier semaphores. Data moves between devices by JAX's collectives and lax.ppermute only.
A program may use at most 192 MiB of HBM per device.

v0:
```python
import jax
import jax.numpy as jnp
from jax import lax
from jax.sharding import PartitionSpec as P

HEADS = 4
SCALE_POWER = -0.5


def shortened(array):
    return jax.tree.map(lambda a: a.astype(jnp.bfloat16) if a.dtype == jnp.float32 else a, array)


def shifted(value, axis, steps):
    count = lax.axis_size(axis)
    first, last = (max(0, -steps), min(count, count - steps))
    return lax.ppermute(value, axis, [(source, source + steps) for source in range(first, last)])


def with_halo(array, sides, width):
    for axis, dim in sides:
        peers, length = (lax.axis_size(axis), array.shape[dim])
        up = [(i, (i + 1) % peers) for i in range(peers - 1)]
        down = [(j, i) for i, j in up]
        last = lax.slice_in_dim(array, length - width, length, axis=dim)
        first = lax.slice_in_dim(array, 0, width, axis=dim)
        before = lax.ppermute(last, axis, up)
        after = lax.ppermute(first, axis, down)
        array = jnp.concatenate([before, array, after], axis=dim)
    return array


def product(pattern, first_op, second_op):
    return jnp.einsum(pattern, first_op, second_op, preferred_element_type=jnp.float32)


def stack_window(extended, tile_cols):
    window_parts = []
    for row_off in range(3):
        for col_off in range(3):
            window_parts.append(extended[row_off, col_off : col_off + tile_cols])
    stacked = jnp.stack(window_parts, axis=1)
    return stacked.reshape((tile_cols, 9 * stacked.shape[2]) + stacked.shape[3:])


def window_keep(row_ok, col_ok, tile_cols, tile_len):
    flag_list = []
    for row_off in range(3):
        for col_off in range(3):
            flag_list.append(
                jnp.logical_and(row_ok[row_off], col_ok[col_off : col_off + tile_cols])
            )
    stacked = jnp.stack(flag_list, axis=1)
    return jnp.repeat(stacked, tile_len, axis=1)


def spread_window(stacked, tile_cols, tile_len):
    window_parts = stacked.reshape((tile_cols, 3, 3, tile_len) + stacked.shape[2:])
    spread_rows = []
    for row_off in range(3):
        gathered = None
        for col_off in range(3):
            placed = jnp.pad(
                window_parts[:, row_off, col_off], ((col_off, 2 - col_off), (0, 0), (0, 0))
            )
            gathered = placed if gathered is None else gathered + placed
        spread_rows.append(gathered)
    return jnp.stack(spread_rows)


def widen_rim(edge_part, axis_pos, length, at_first):
    expanded = jnp.expand_dims(edge_part, axis_pos)
    pad_spec = [(0, 0)] * expanded.ndim
    pad_spec[axis_pos] = (0, length - 1) if at_first else (length - 1, 0)
    return jnp.pad(expanded, pad_spec)


def attend_row(query_row, key_ext, value_ext, visible, head_count):
    tile_cols, tile_len, feature_width = query_row.shape
    head_dim = feature_width // head_count
    score_scale = head_dim**SCALE_POWER
    query_heads = query_row.reshape(tile_cols, tile_len, head_count, head_dim)
    key_heads = stack_window(key_ext, tile_cols).reshape(
        tile_cols, 9 * tile_len, head_count, head_dim
    )
    value_heads = stack_window(value_ext, tile_cols).reshape(
        tile_cols, 9 * tile_len, head_count, head_dim
    )
    scores = product("jqhd,jkhd->jhqk", query_heads, key_heads) * score_scale
    scores = jnp.where(visible[:, None, None, :], scores, -1e30)
    row_max = jnp.max(scores, axis=-1, keepdims=True)
    log_norm = row_max + jnp.log(jnp.sum(jnp.exp(scores - row_max), axis=-1, keepdims=True))
    soft_probs = jnp.exp(scores - log_norm).astype(jnp.bfloat16)
    attended = product("jhqk,jkhd->jqhd", soft_probs, value_heads)
    attended = attended.reshape(tile_cols, tile_len, feature_width).astype(jnp.bfloat16)
    return (attended, soft_probs, log_norm[..., 0])


def query_back(query_row, key_ext, value_ext, attended, grad_attn, soft_probs, head_count):
    tile_cols, tile_len, feature_width = query_row.shape
    head_dim = feature_width // head_count
    score_scale = head_dim**SCALE_POWER
    attended_heads = attended.astype(jnp.float32).reshape(tile_cols, tile_len, head_count, head_dim)
    grad_heads = grad_attn.reshape(tile_cols, tile_len, head_count, head_dim)
    row_delta = jnp.sum(attended_heads * grad_heads.astype(jnp.float32), axis=-1)
    row_delta = jnp.transpose(row_delta, (0, 2, 1))
    value_heads = stack_window(value_ext, tile_cols).reshape(
        tile_cols, 9 * tile_len, head_count, head_dim
    )
    prob_grad = product("jqhd,jkhd->jhqk", grad_heads, value_heads)
    score_grad = (soft_probs.astype(jnp.float32) * (prob_grad - row_delta[..., None])).astype(
        jnp.bfloat16
    )
    key_heads = stack_window(key_ext, tile_cols).reshape(
        tile_cols, 9 * tile_len, head_count, head_dim
    )
    query_grad = product("jhqk,jkhd->jqhd", score_grad, key_heads) * score_scale
    query_grad = query_grad.reshape(tile_cols, tile_len, feature_width)
    query_heads = query_row.reshape(tile_cols, tile_len, head_count, head_dim)
    key_part = (product("jhqk,jqhd->jkhd", score_grad, query_heads) * score_scale).reshape(
        tile_cols, 9 * tile_len, feature_width
    )
    value_part = product("jhqk,jqhd->jkhd", soft_probs, grad_heads).reshape(
        tile_cols, 9 * tile_len, feature_width
    )
    return (
        query_grad,
        row_delta,
        spread_window(key_part, tile_cols, tile_len),
        spread_window(value_part, tile_cols, tile_len),
    )


def send_rows(edge_part, offset):
    return shifted(shortened(edge_part), "ha", offset).astype(edge_part.dtype)


def send_columns(edge_part, offset):
    return shifted(shortened(edge_part), "wa", offset).astype(edge_part.dtype)


def on_device(query_in, key_in, value_in, grad_out, out_weight):
    clip_count, tile_rows, tile_cols, tile_len, feature_width = query_in.shape
    model_width = grad_out.shape[-1]
    head_count = HEADS
    row_first = lax.axis_index("ha") * tile_rows
    col_first = lax.axis_index("wa") * tile_cols
    all_rows = tile_rows * lax.axis_size("ha")
    all_cols = tile_cols * lax.axis_size("wa")
    row_global = row_first - 1 + jnp.arange(tile_rows + 2, dtype=jnp.int32)
    row_flags = jnp.logical_and(row_global >= 0, row_global < all_rows)
    col_global = col_first - 1 + jnp.arange(tile_cols + 2, dtype=jnp.int32)
    col_ok = jnp.logical_and(col_global >= 0, col_global < all_cols)
    full_weight = lax.all_gather(out_weight, "dp", axis=0, tiled=True)
    flat_grad = grad_out.reshape(-1, model_width)
    grad_attn = lax.dot_general(
        flat_grad, full_weight, (((1,), (1,)), ((), ())), preferred_element_type=jnp.float32
    )
    grad_attn = grad_attn.astype(jnp.bfloat16).reshape(query_in.shape)
    extended = with_halo(jnp.stack([key_in, value_in]), (("ha", 2), ("wa", 3)), 1)
    key_ext_all = extended[0]
    value_ext_all = extended[1]
    row_total = clip_count * tile_rows
    flat_rows = jnp.arange(row_total, dtype=jnp.int32)
    query_rows = query_in.reshape(row_total, tile_cols, tile_len, feature_width)
    grad_rows = grad_attn.reshape(row_total, tile_cols, tile_len, feature_width)

    def row_window(extended_all):
        return extended_all[0]

    def row_keep():
        return window_keep(row_flags, col_ok, tile_cols, tile_len)

    def forward_row(inputs):
        query_row, flat_index = inputs
        return attend_row(
            query_row, row_window(key_ext_all), row_window(value_ext_all), row_keep(), head_count
        )

    attended, soft_probs, log_norm = lax.map(forward_row, (query_rows, flat_rows))
    flat_attn = attended.reshape(-1, feature_width)
    outcome = jnp.dot(flat_attn, full_weight, preferred_element_type=jnp.float32).astype(
        jnp.bfloat16
    )
    outcome = outcome.reshape(clip_count, tile_rows, tile_cols, tile_len, model_width)

    def query_side(inputs):
        query_row, grad_row, attended_row, probs_row, flat_index = inputs
        query_grad, row_delta, key_part, value_part = query_back(
            query_row,
            row_window(key_ext_all),
            row_window(value_ext_all),
            attended_row,
            grad_row,
            probs_row,
            head_count,
        )
        return (query_grad, jnp.stack([key_part, value_part]))

    query_grad, ext_parts = lax.map(
        query_side, (query_rows, grad_rows, attended, soft_probs, flat_rows)
    )
    ext_parts = ext_parts.reshape(
        clip_count, tile_rows, 2, 3, tile_cols + 2, tile_len, feature_width
    )
    padded_grad = None
    for row_off in range(3):
        placed = jnp.pad(
            ext_parts[:, :, :, row_off],
            ((0, 0), (row_off, 2 - row_off), (0, 0), (0, 0), (0, 0), (0, 0)),
        )
        padded_grad = placed if padded_grad is None else padded_grad + placed
    from_below = send_rows(padded_grad[:, 0], -1)
    from_above = send_rows(padded_grad[:, tile_rows + 1], 1)
    middle = padded_grad[:, 1 : tile_rows + 1]
    middle = (
        middle
        + widen_rim(from_below, 1, tile_rows, False)
        + widen_rim(from_above, 1, tile_rows, True)
    )
    from_right = send_columns(middle[:, :, :, 0], -1)
    from_left = send_columns(middle[:, :, :, tile_cols + 1], 1)
    core_part = middle[:, :, :, 1 : tile_cols + 1]
    core_part = (
        core_part
        + widen_rim(from_right, 3, tile_cols, False)
        + widen_rim(from_left, 3, tile_cols, True)
    )
    key_grad = core_part[:, :, 0]
    value_grad = core_part[:, :, 1]
    query_grad = query_grad.reshape(query_in.shape)
    row_share = feature_width // lax.axis_size("dp")
    local_term = lax.dot_general(
        flat_attn, flat_grad, (((0,), (0,)), ((), ())), preferred_element_type=jnp.float32
    )
    summed = lax.psum(local_term, ("dp", "ha", "wa"))
    weight_grad = lax.dynamic_slice_in_dim(summed, lax.axis_index("dp") * row_share, row_share, 0)
    return (outcome, query_grad, key_grad, value_grad, weight_grad)


def solution(mesh):
    return jax.shard_map(
        on_device,
        mesh=mesh,
        in_specs=(
            P("dp", "ha", "wa", None, None),
            P("dp", "ha", "wa", None, None),
            P("dp", "ha", "wa", None, None),
            P("dp", "ha", "wa", None, None),
            P("dp", None),
        ),
        out_specs=(
            P("dp", "ha", "wa", None, None),
            P("dp", "ha", "wa", None, None),
            P("dp", "ha", "wa", None, None),
            P("dp", "ha", "wa", None, None),
            P("dp", None),
        ),
        check_vma=False,
    )
```

profile of v0, /device:TPU:0, one launch (start us, length us, event | category | flops | bytes accessed | tf_op | source)
XLA Modules:
  0.0 480.3 jit_solution(6171080770053422806)
XLA Ops:
  10.5 5.6 %collective-permute-start = (bf16[2,1,1,1,384,512]{5,4,3,2,1,0:T(8,128)(2,1)S(1)}, bf16[2,1,1,1,384,512]{5,4,3,2,1,0:T(8,128)(2,1)S(1)}, u32[]{:S(2)}, u32[]{:S(2)}) collective-permute-start(bf16[2,1,1,1,384,512]{5,4,3,2,1,0:T(8,128)(2,1)S(1)} %pad_maximum_fusion.4), channel_id=1, source_target_pairs={{0,4},{4,8},{8,12},{1,5},{5,9},{9,13},{2,6},{6,10},{10,14},{3,7},{... | collective-permute-start | bytes 2359304 | tf_op jit(solution)/shard_map/ppermute | solution.py:27
  16.1 15.6 %collective-permute-done.1 = bf16[2,1,1,1,384,512]{5,4,3,2,1,0:T(8,128)(2,1)S(1)} collective-permute-done((bf16[2,1,1,1,384,512]{5,4,3,2,1,0:T(8,128)(2,1)S(1)}, bf16[2,1,1,1,384,512]{5,4,3,2,1,0:T(8,128)(2,1)S(1)}, u32[]{:S(2)}, u32[]{:S(2)}) %collective-permute-start.1) | collective-permute-done | bytes 786464 | tf_op jit(solution)/shard_map/ppermute | solution.py:28
  37.2 4.5 collective-permute-start.2
  71.5 7.2 %reshape.242 = bf16[3456,4,128]{2,1,0:T(4,128)(2,1)} reshape(bf16[1,9,384,512]{3,2,1,0:T(8,128)(2,1)} %pad_maximum_fusion.2) | data formatting | bytes 7077888 | tf_op jit(solution)/shard_map/reshape.31
  78.7 6.9 %copy.102 = bf16[3456,4,128]{0,2,1:T(8,128)(2,1)} copy(bf16[3456,4,128]{2,1,0:T(4,128)(2,1)} %reshape.242) | data formatting | bytes 7077888 | tf_op jit(solution)/shard_map/reshape.31
  85.6 7.5 %bitcast_reduce_fusion = (f32[4,384]{1,0:T(4,128)S(1)}, f32[4,3456,384]{2,1,0:T(8,128)S(1)}) fusion(pred[3456]{0:T(1024)(128)(4,1)S(1)} %broadcast_in_dim.69, bf16[3456,4,128]{0,2,1:T(8,128)(2,1)} %copy.102, bf16[384,4,128]{2,1,0:T(4,128)(2,1)S(1)} %copy-done.9), kind=kOutput, calls=%fused_computation.2 | convolution fusion | flops 1374878208 | bytes 25175424 | tf_op jit(solution)/shard_map/while/body/eval_jaxpr/jqhd,jkhd->jhqk/dot_general | solution.py:34
  93.1 5.7 %fusion.1 = f32[4,384]{1,0:T(4,128)S(1)} fusion(f32[4,3456,384]{2,1,0:T(8,128)S(1)} %get-tuple-element.125, f32[4,384]{1,0:T(4,128)S(1)} %get-tuple-element.124, pred[3456]{0:T(1024)(128)(4,1)S(1)} %broadcast_in_dim.69), kind=kLoop, calls=%fused_computation.4 | loop fusion | flops 21232128 | bytes 21249408 | tf_op jit(solution)/shard_map/while/body/eval_jaxpr/reduce_sum | solution.py:92
  98.8 7.5 %fusion.3 = bf16[4,384,3456]{1,2,0:T(8,128)(2,1)} fusion(f32[4,3456,384]{2,1,0:T(8,128)S(1)} %get-tuple-element.125, f32[4,384]{1,0:T(4,128)S(1)} %log_add_fusion, pred[3456]{0:T(1024)(128)(4,1)S(1)} %broadcast_in_dim.69), kind=kLoop, calls=%fused_computation.6 | loop fusion | flops 21233664 | bytes 31860096 | tf_op jit(solution)/shard_map/while/body/eval_jaxpr/convert_element_type | solution.py:93
  108.2 7.4 %reshape.241 = bf16[3456,4,128]{2,1,0:T(4,128)(2,1)} reshape(bf16[1,9,384,512]{3,2,1,0:T(8,128)(2,1)} %pad_maximum_fusion.1) | data formatting | bytes 7077888 | tf_op jit(solution)/shard_map/reshape.41
  115.6 10.2 %convolution_bitcast_fusion = f32[1,3456,4,128]{1,3,2,0:T(8,128)} fusion(bf16[384,4,128]{0,2,1:T(8,128)(2,1)S(1)} %bitcast.185, bf16[4,384,3456]{1,2,0:T(8,128)(2,1)} %fusion.3), kind=kOutput, calls=%fused_computation.15 | convolution fusion | flops 1358954496 | bytes 18087936 | tf_op jit(solution)/shard_map/while/body/eval_jaxpr/jhqk,jqhd->jkhd/dot_general | solution.py:34
  125.8 6.3 %multiply_reduce_fusion = (f32[384,4]{0,1:T(4,128)S(1)}, bf16[4,128,384]{2,1,0:T(8,128)(2,1)S(1)}) fusion(f32[1,384,4,128]{1,3,2,0:T(8,128)S(1)} %bitcast.195, bf16[4,384,3456]{1,2,0:T(8,128)(2,1)} %fusion.3, bf16[3456,4,128]{2,1,0:T(4,128)(2,1)S(1)} %copy-done.2), kind=kOutput, calls=%fused_computation.75 | convolution fusion | flops 1359739392 | bytes 15341568 | tf_op jit(solution)/shard_map/while/body/eval_jaxpr/jhqk,jkhd->jqhd/dot_general | solution.py:34
  132.1 12.1 %multiply_convert_fusion = bf16[4,384,3456]{1,2,0:T(8,128)(2,1)} fusion(bf16[4,384,3456]{1,2,0:T(8,128)(2,1)} %fusion.3, bf16[384,4,128]{0,2,1:T(8,128)(2,1)S(1)} %bitcast.186, f32[4,384]{1,0:T(4,128)S(1)} %bitcast.197, bf16[3456,4,128]{2,1,0:T(4,128)(2,1)} %reshape.241), kind=kOutput, calls=%fused_computation.7 | convolution fusion | flops 1380188160 | bytes 25171968 | tf_op jit(solution)/shard_map/while/body/eval_jaxpr/jqhd,jkhd->jhqk/dot_general | solution.py:34
  144.2 9.2 %copy.108 = f32[1,3456,4,128]{3,2,0,1:T(4,128)} copy(f32[1,3456,4,128]{1,3,2,0:T(8,128)} %convolution_bitcast_fusion) | data formatting | bytes 14155776 | tf_op jit(solution)/shard_map/while/body/eval_jaxpr/jhqk,jqhd->jkhd/transpose | solution.py:34
  153.4 8.4 %slice_bitcast_fusion.23 = (f32[1,384,512]{2,0,1:T(1,128)S(1)}, f32[1,384,512]{2,0,1:T(1,128)}, f32[1,384,512]{2,0,1:T(1,128)}, f32[1,384,512]{2,0,1:T(1,128)}, ...) fusion(f32[1,3,3,384,512]{4,0,3,2,1:T(1,128)} %bitcast.183), kind=kLoop, calls=%fused_computation.64 | loop fusion | bytes 14155776 | tf_op jit(solution)/shard_map/while/body/eval_jaxpr/squeeze | solution.py:64
  164.7 15.1 %copy.105 = f32[1,3456,4,128]{3,2,0,1:T(4,128)S(1)} copy(f32[1,3456,4,128]{3,1,2,0:T(8,128)S(1)} %multiply_bitcast_fusion) | data formatting | bytes 14155776 | tf_op jit(solution)/shard_map/while/body/eval_jaxpr/mul | solution.py:120
  179.8 4.1 slice_bitcast_fusion.32
  193.5 9.7 %maximum_bitcast_fusion.2 = f32[1,3,3,384,512]{4,2,3,1,0:T(4,128)} fusion(f32[1,3,384,512]{3,1,2,0:T(4,128)} %add_bitcast_fusion, f32[1,3,384,512]{3,1,2,0:T(4,128)} %add_bitcast_fusion.1, f32[1,3,384,512]{3,1,2,0:T(4,128)} %add_bitcast_fusion.2), kind=kLoop, calls=%fused_computation.12 | loop fusion | flops 3538944 | bytes 14155776 | tf_op jit(solution)/shard_map/while/body/eval_jaxpr/stack | solution.py:198
  203.2 4.5 add_bitcast_fusion.3
  214.5 9.7 %maximum_bitcast_fusion.1 = f32[1,3,3,384,512]{4,2,3,1,0:T(4,128)} fusion(f32[1,3,384,512]{3,1,2,0:T(4,128)} %add_bitcast_fusion.3, f32[1,3,384,512]{3,1,2,0:T(4,128)} %add_bitcast_fusion.4, f32[1,3,384,512]{3,1,2,0:T(4,128)} %add_bitcast_fusion.5), kind=kLoop, calls=%fused_computation.11 | loop fusion | flops 3538944 | bytes 14155776 | tf_op jit(solution)/shard_map/while/body/eval_jaxpr/stack | solution.py:198
  224.2 10.5 %maximum_bitcast_fusion = f32[1,1,2,3,3,384,512]{6,4,5,3,2,1,0:T(4,128)S(1)} fusion(f32[1,3,3,384,512]{4,2,3,1,0:T(4,128)} %maximum_bitcast_fusion.2, f32[1,3,3,384,512]{4,2,3,1,0:T(4,128)} %maximum_bitcast_fusion.1), kind=kLoop, calls=%fused_computation.9 | loop fusion | flops 3538944 | bytes 28311552 | tf_op jit(solution)/shard_map/reshape | solution.py:203
  234.6 7.7 %slice_bitcast_fusion.2 = (f32[1,1,2,3,384,512]{5,3,4,2,1,0:T(4,128)}, f32[1,1,2,3,384,512]{5,3,4,2,1,0:T(4,128)}, f32[1,1,2,3,384,512]{5,3,4,2,1,0:T(4,128)}) fusion(f32[1,1,2,3,3,384,512]{6,4,5,3,2,1,0:T(4,128)S(1)} %maximum_bitcast_fusion), kind=kLoop, calls=%fused_computation.20 | loop fusion | bytes 28311552 | tf_op jit(solution)/shard_map/squeeze | solution.py:209
  242.3 18.2 %pad_add_fusion = (f32[1,3,2,3,384,512]{5,3,4,2,1,0:T(4,128)}, bf16[1,3,2,3,384,512]{5,3,4,2,1,0:T(4,128)(2,1)S(1)}) fusion(f32[1,1,2,3,384,512]{5,3,4,2,1,0:T(4,128)} %get-tuple-element.86, f32[1,1,2,3,384,512]{5,3,4,2,1,0:T(4,128)} %get-tuple-element.87, f32[1,1,2,3,384,512]{5,3,4,2,1,0:T(4,128)} %get-tuple-element.85), kind=kLoop, calls=%fused_computation.10 | loop fusion | flops 10616832 | bytes 35389440 | tf_op jit(solution)/shard_map/add | solution.py:212
  264.8 4.8 collective-permute-start.5
  272.8 4.4 fusion.9
  277.2 63.5 %collective-permute-done.5 = bf16[1,2,3,384,512]{4,3,2,1,0:T(8,128)(2,1)} collective-permute-done((bf16[1,2,3,384,512]{4,3,2,1,0:T(8,128)(2,1)}, bf16[1,2,3,384,512]{4,3,2,1,0:T(8,128)(2,1)}, u32[]{:S(2)}, u32[]{:S(2)}) %collective-permute-start.5) | collective-permute-done | bytes 2359328 | tf_op jit(solution)/shard_map/ppermute | solution.py:17
  340.7 12.7 %collective-permute-done.4 = bf16[1,2,3,384,512]{4,3,2,1,0:T(8,128)(2,1)} collective-permute-done((bf16[1,2,3,384,512]{4,3,2,1,0:T(8,128)(2,1)}, bf16[1,2,3,384,512]{4,3,2,1,0:T(8,128)(2,1)}, u32[]{:S(2)}, u32[]{:S(2)}) %collective-permute-start.4) | collective-permute-done | bytes 2359328 | tf_op jit(solution)/shard_map/ppermute | solution.py:17
  353.5 10.7 %fusion.24 = (bf16[1,1,2,3,384,512]{5,3,4,2,1,0:T(4,128)(2,1)S(1)}, f32[1,1,2,3,384,512]{5,3,4,2,1,0:T(4,128)}) fusion(bf16[1,2,3,384,512]{4,3,2,1,0:T(8,128)(2,1)} %collective-permute-done.5, bf16[1,2,3,384,512]{4,3,2,1,0:T(8,128)(2,1)} %collective-permute-done.4, f32[1,3,2,3,384,512]{5,3,4,2,1,0:T(4,128)} %get-tuple-element.83), kind=kLoop, calls=%fused_computation.84 | loop fusion | flops 5898240 | bytes 16515072 | tf_op jit(solution)/shard_map/convert.6
  367.6 6.8 %collective-permute-start.7 = (bf16[1,1,2,384,512]{4,0,3,2,1:T(2,128)(2,1)}, bf16[1,1,2,384,512]{4,0,3,2,1:T(2,128)(2,1)}, u32[]{:S(2)}, u32[]{:S(2)}) collective-permute-start(bf16[1,1,2,384,512]{4,0,3,2,1:T(2,128)(2,1)} %get-tuple-element.115), channel_id=1, source_target_pairs={{0,1},{1,2},{2,3},{4,5},{5,6},{6,7},{8,9},{9,10},{10,11},{12,13},{... | collective-permute-start | bytes 2359304 | tf_op jit(solution)/shard_map/ppermute | solution.py:17
  375.7 7.2 %convolution_multiply_fusion = f32[4,128,384]{2,1,0:T(8,128)} fusion(bf16[3456,4,128]{0,2,1:T(8,128)(2,1)S(1)} %copy-done.3, bf16[4,384,3456]{1,2,0:T(8,128)(2,1)} %multiply_convert_fusion), kind=kOutput, calls=%fused_computation.45 | convolution fusion | flops 1359151104 | bytes 14942208 | tf_op jit(solution)/shard_map/while/body/eval_jaxpr/jhqk,jkhd->jqhd/dot_general | solution.py:34
  385.2 4.7 fusion.5
  389.9 7.0 %fusion.13 = f32[1,1,2,1,384,512]{5,3,4,2,1,0:T(1,128)S(1)} fusion(f32[1,1,2,3,384,512]{5,3,4,2,1,0:T(4,128)} %get-tuple-element.82, bf16[1,1,2,384,512]{4,0,3,2,1:T(2,128)(2,1)} %collective-permute-done.7, bf16[1,1,2,384,512]{4,0,3,2,1:T(2,128)(2,1)} %collective-permute-done.6), kind=kLoop, calls=%fused_computation.44 | loop fusion | flops 1572864 | bytes 4718592 | tf_op jit(solution)/shard_map/add | solution.py:225
  399.9 69.5 %all-reduce.23.cloned.1.call-done = f32[512,3072]{1,0:T(8,128)} async-done(((f32[512,3072]{1,0:T(8,128)}), f32[512,3072]{1,0:T(8,128)}) %all-reduce.23.cloned.1.call-update) | async-done | bytes 6291472 | tf_op jit(solution)/shard_map/psum | solution.py:236
  (98 shorter events, 69.7 us)
Async XLA Ops:
  7.2 50.0 %copy-start = (bf16[1,1,1,384,3072]{4,3,2,1,0:T(8,128)(2,1)S(1)}, bf16[1,1,1,384,3072]{4,3,2,1,0:T(8,128)(2,1)}, u32[]{:S(2)}) copy-start(bf16[1,1,1,384,3072]{4,3,2,1,0:T(8,128)(2,1)} %param.8) | copy-start | bytes 7077892
  7.2 50.0 %all-gather.2.cloned.1.call-start = ((), (), s32[]{:S(2)}) async-start(), calls=%async_computation | async-start | bytes 4718592 | tf_op jit(solution)/shard_map/all_gather | solution.py:154
  7.9 46.0 %copy-start.25 = (bf16[1,1,1,384,512]{4,3,2,1,0:T(8,128)(2,1)S(1)}, bf16[1,1,1,384,512]{4,3,2,1,0:T(8,128)(2,1)}, u32[]{:S(2)}) copy-start(bf16[1,1,1,384,512]{4,3,2,1,0:T(8,128)(2,1)} %param.5) | copy-start | bytes 1179652
  7.9 461.5 %all-reduce.23.cloned.1.call-start = ((), (), s32[]{:S(2)}) async-start(), calls=%async_computation.1 | async-start | bytes 12582912 | tf_op jit(solution)/shard_map/psum | solution.py:236
  9.2 22.5 %collective-permute-start.1 = (bf16[2,1,1,1,384,512]{5,4,3,2,1,0:T(8,128)(2,1)S(1)}, bf16[2,1,1,1,384,512]{5,4,3,2,1,0:T(8,128)(2,1)S(1)}, u32[]{:S(2)}, u32[]{:S(2)}) collective-permute-start(bf16[2,1,1,1,384,512]{5,4,3,2,1,0:T(8,128)(2,1)S(1)} %pad_maximum_fusion.4), channel_id=1, source_target_pairs={{4,0},{8,4},{12,8},{5,1},{9,5},{13,9},{6,2},{10,6},{14,10},{7,3},{... | collective-permute-start | bytes 2359304 | tf_op jit(solution)/shard_map/ppermute | solution.py:28
  10.5 22.4 %collective-permute-start = (bf16[2,1,1,1,384,512]{5,4,3,2,1,0:T(8,128)(2,1)S(1)}, bf16[2,1,1,1,384,512]{5,4,3,2,1,0:T(8,128)(2,1)S(1)}, u32[]{:S(2)}, u32[]{:S(2)}) collective-permute-start(bf16[2,1,1,1,384,512]{5,4,3,2,1,0:T(8,128)(2,1)S(1)} %pad_maximum_fusion.4), channel_id=1, source_target_pairs={{0,4},{4,8},{8,12},{1,5},{5,9},{9,13},{2,6},{6,10},{10,14},{3,7},{... | collective-permute-start | bytes 2359304 | tf_op jit(solution)/shard_map/ppermute | solution.py:27
  35.9 27.6 %collective-permute-start.3 = (bf16[2,1,3,1,384,512]{5,4,3,2,1,0:T(8,128)(2,1)}, bf16[2,1,3,1,384,512]{5,4,3,2,1,0:T(8,128)(2,1)}, u32[]{:S(2)}, u32[]{:S(2)}) collective-permute-start(bf16[2,1,3,1,384,512]{5,4,3,2,1,0:T(8,128)(2,1)} %pad_maximum_fusion.3), channel_id=1, source_target_pairs={{1,0},{2,1},{3,2},{5,4},{6,5},{7,6},{9,8},{10,9},{11,10},{13,12},{... | collective-permute-start | bytes 7077896 | tf_op jit(solution)/shard_map/ppermute | solution.py:28
  37.2 26.3 %collective-permute-start.2 = (bf16[2,1,3,1,384,512]{5,4,3,2,1,0:T(8,128)(2,1)}, bf16[2,1,3,1,384,512]{5,4,3,2,1,0:T(8,128)(2,1)}, u32[]{:S(2)}, u32[]{:S(2)}) collective-permute-start(bf16[2,1,3,1,384,512]{5,4,3,2,1,0:T(8,128)(2,1)} %pad_maximum_fusion.3), channel_id=1, source_target_pairs={{0,1},{1,2},{2,3},{4,5},{5,6},{6,7},{8,9},{9,10},{10,11},{12,13},{... | collective-permute-start | bytes 7077896 | tf_op jit(solution)/shard_map/ppermute | solution.py:27
  54.9 8.7 %copy-start.7 = (bf16[1,1,1,384,512]{4,3,2,1,0:T(8,128)(2,1)S(1)}, bf16[1,1,1,384,512]{4,3,2,1,0:T(8,128)(2,1)}, u32[]{:S(2)}) copy-start(bf16[1,1,1,384,512]{4,3,2,1,0:T(8,128)(2,1)} %param.7) | copy-start | bytes 1179652
  54.9 8.7 %copy-start.8 = (bf16[1,1,1,384,512]{4,3,2,1,0:T(8,128)(2,1)S(1)}, bf16[1,1,1,384,512]{4,3,2,1,0:T(8,128)(2,1)}, u32[]{:S(2)}) copy-start(bf16[1,1,1,384,512]{4,3,2,1,0:T(8,128)(2,1)} %param.6) | copy-start | bytes 1179652
  78.7 6.9 %copy-start.9 = (bf16[384,4,128]{2,1,0:T(4,128)(2,1)S(1)}, bf16[384,4,128]{2,1,0:T(4,128)(2,1)}, u32[]{:S(2)}) copy-start(bf16[384,4,128]{2,1,0:T(4,128)(2,1)} %reshape.243) | copy-start | bytes 1179652
  98.7 7.5 %copy-start.4 = (bf16[1,3,384,512]{3,2,1,0:T(8,128)(2,1)S(1)}, bf16[1,3,384,512]{3,2,1,0:T(8,128)(2,1)}, u32[]{:S(2)}) copy-start(bf16[1,3,384,512]{3,2,1,0:T(8,128)(2,1)} %get-tuple-element.108) | copy-start | bytes 3538948
  98.8 7.5 %copy-start.5 = (bf16[1,3,384,512]{3,2,1,0:T(8,128)(2,1)S(1)}, bf16[1,3,384,512]{3,2,1,0:T(8,128)(2,1)}, u32[]{:S(2)}) copy-start(bf16[1,3,384,512]{3,2,1,0:T(8,128)(2,1)} %get-tuple-element.112) | copy-start | bytes 3538948
  98.8 7.5 %copy-start.6 = (bf16[1,3,384,512]{3,2,1,0:T(8,128)(2,1)S(1)}, bf16[1,3,384,512]{3,2,1,0:T(8,128)(2,1)}, u32[]{:S(2)}) copy-start(bf16[1,3,384,512]{3,2,1,0:T(8,128)(2,1)} %get-tuple-element.113) | copy-start | bytes 3538948
  115.6 10.2 %copy-start.2 = (bf16[3456,4,128]{2,1,0:T(4,128)(2,1)S(1)}, bf16[3456,4,128]{2,1,0:T(4,128)(2,1)}, u32[]{:S(2)}) copy-start(bf16[3456,4,128]{2,1,0:T(4,128)(2,1)} %reshape.241) | copy-start | bytes 10616836
  115.6 10.2 %copy-start.10 = (f32[384,512]{0,1:T(8,128)S(1)}, f32[384,512]{0,1:T(8,128)}, u32[]{:S(2)}) copy-start(f32[384,512]{0,1:T(8,128)} %copy.100) | copy-start | bytes 2359300
  153.4 8.4 %copy-start.1 = (bf16[4,384,3456]{1,2,0:T(8,128)(2,1)S(1)}, bf16[4,384,3456]{1,2,0:T(8,128)(2,1)}, u32[]{:S(2)}) copy-start(bf16[4,384,3456]{1,2,0:T(8,128)(2,1)} %multiply_convert_fusion) | copy-start | bytes 31850500
  179.8 4.2 copy-start.21
  179.8 4.2 copy-start.22
  179.8 4.2 copy-start.23
  184.0 3.2 copy-start.20
  203.2 4.5 copy-start.16
  203.2 4.5 copy-start.17
  203.2 4.5 copy-start.18
  207.7 3.6 copy-start.13
  207.7 3.6 copy-start.14
  207.7 3.6 copy-start.15
  264.8 76.0 %collective-permute-start.5 = (bf16[1,2,3,384,512]{4,3,2,1,0:T(8,128)(2,1)}, bf16[1,2,3,384,512]{4,3,2,1,0:T(8,128)(2,1)}, u32[]{:S(2)}, u32[]{:S(2)}) collective-permute-start(bf16[1,2,3,384,512]{4,3,2,1,0:T(8,128)(2,1)} %copy.113), channel_id=1, source_target_pairs={{0,4},{4,8},{8,12},{1,5},{5,9},{9,13},{2,6},{6,10},{10,14},{3,7},{... | collective-permute-start | bytes 7077896 | tf_op jit(solution)/shard_map/ppermute | solution.py:17
  271.5 82.0 %collective-permute-start.4 = (bf16[1,2,3,384,512]{4,3,2,1,0:T(8,128)(2,1)}, bf16[1,2,3,384,512]{4,3,2,1,0:T(8,128)(2,1)}, u32[]{:S(2)}, u32[]{:S(2)}) collective-permute-start(bf16[1,2,3,384,512]{4,3,2,1,0:T(8,128)(2,1)} %copy.111), channel_id=1, source_target_pairs={{4,0},{8,4},{12,8},{5,1},{9,5},{13,9},{6,2},{10,6},{14,10},{7,3},{... | collective-permute-start | bytes 7077896 | tf_op jit(solution)/shard_map/ppermute | solution.py:17
  364.2 11.5 %copy-start.3 = (bf16[3456,4,128]{0,2,1:T(8,128)(2,1)S(1)}, bf16[3456,4,128]{0,2,1:T(8,128)(2,1)}, u32[]{:S(2)}) copy-start(bf16[3456,4,128]{0,2,1:T(8,128)(2,1)} %copy.102) | copy-start | bytes 10616836
  367.6 22.3 %collective-permute-start.7 = (bf16[1,1,2,384,512]{4,0,3,2,1:T(2,128)(2,1)}, bf16[1,1,2,384,512]{4,0,3,2,1:T(2,128)(2,1)}, u32[]{:S(2)}, u32[]{:S(2)}) collective-permute-start(bf16[1,1,2,384,512]{4,0,3,2,1:T(2,128)(2,1)} %get-tuple-element.115), channel_id=1, source_target_pairs={{0,1},{1,2},{2,3},{4,5},{5,6},{6,7},{8,9},{9,10},{10,11},{12,13},{... | collective-permute-start | bytes 2359304 | tf_op jit(solution)/shard_map/ppermute | solution.py:17
  374.4 15.5 %collective-permute-start.6 = (bf16[1,1,2,384,512]{4,0,3,2,1:T(2,128)(2,1)}, bf16[1,1,2,384,512]{4,0,3,2,1:T(2,128)(2,1)}, u32[]{:S(2)}, u32[]{:S(2)}) collective-permute-start(bf16[1,1,2,384,512]{4,0,3,2,1:T(2,128)(2,1)} %get-tuple-element.114), channel_id=1, source_target_pairs={{1,0},{2,1},{3,2},{5,4},{6,5},{7,6},{9,8},{10,9},{11,10},{13,12},{... | collective-permute-start | bytes 2359304 | tf_op jit(solution)/shard_map/ppermute | solution.py:17
  (4 other events, 8.2 us)
Sparse Core Ops, SparseCore 0:
  9.5 47.6 all-gather.1
  277.4 191.9 all-reduce.22
where the time goes:
time: 490 us; the launch traced here: 480 us
  waiting for transfers between devices  166 us (34%)
  other arithmetic  112 us (23%)
  local copies, waits for them, and re-layouts  91.6 us (19%)
  matrix products  58.7 us (12%)
  starting transfers between devices  26.9 us (5%)
  between operations  26 us (5%)
    ppermute x4, waiting for transfers between devices, shifted(): lax.ppermute(value, axis, [(source, source + steps) for source in range(f...  76.2 us
    psum x1, waiting for transfers between devices, on_device(): summed = lax.psum(local_term, ('dp', 'ha', 'wa'))  69.5 us
    dot_general x6, matrix products, product(): jnp.einsum(pattern, first_op, second_op, preferred_element_type=jnp.float32)  46.2 us
    another operation x5, local copies, waits for them, and re-layouts  23.5 us
    another operation x6, other arithmetic, spread_window(): return jnp.stack(spread_rows)  20.8 us
    another operation x2, other arithmetic, query_side(): return (query_grad, jnp.stack([key_part, value_part]))  19.3 us
    add x1, other arithmetic, on_device(): padded_grad = placed if padded_grad is None else padded_grad + placed  18.2 us
    ppermute x2, waiting for transfers between devices, with_halo(): after = lax.ppermute(first, axis, down)  15.6 us
  transfers between devices with their start and end apart: 10, of which 6 were waited for; matrix products, arithmetic and copies ran while one was open for 12% of the time, Pallas kernels for 0%

commit v1 on v0

--- a/solution.py
+++ b/solution.py
@@ -233,7 +233,7 @@
     local_term = lax.dot_general(
         flat_attn, flat_grad, (((0,), (0,)), ((), ())), preferred_element_type=jnp.float32
     )
-    summed = lax.psum(local_term, ("dp", "ha", "wa"))
+    summed = lax.psum(lax.psum(local_term, "dp"), ("ha", "wa"))
     weight_grad = lax.dynamic_slice_in_dim(summed, lax.axis_index("dp") * row_share, row_share, 0)
     return (outcome, query_grad, key_grad, value_grad, weight_grad)
 

time: 490 us -> 522 us (1.065)
  waiting for transfers between devices: 166 us -> 191 us
  local copies, waits for them, and re-layouts: 91.6 us -> 104 us
  starting transfers between devices: 26.9 us -> 20.8 us
    psum x1 -> x2, waiting for transfers between devices: 69.5 us -> 171 us  [on_device(): summed = lax.psum(lax.psum(local_term, 'dp'), ('ha', 'wa'))]
    ppermute x4, waiting for transfers between devices: 76.2 us -> 0.01 us  [shifted(): lax.ppermute(value, axis, [(source, source + steps) for source in range(f...]
    mul x1, local copies, waits for them, and re-layouts: 15.1 us -> 25.5 us  [query_back(): product('jhqk,jqhd->jkhd', score_grad, query_heads) * score_scale]
    ppermute x4, starting transfers between devices: 14.1 us -> 8.01 us  [shifted(): lax.ppermute(value, axis, [(source, source + steps) for source in range(f...]
  transfers between devices with their start and end apart: 10 -> 11, of which waited for: 6 -> 5; matrix products, arithmetic and copies ran while one was open for 12% -> 26% of each run, Pallas kernels for 0% -> 0%
where the time goes in v1:
time: 522 us; the launch traced here: 513 us
  waiting for transfers between devices  191 us (37%)
  other arithmetic  114 us (22%)
  local copies, waits for them, and re-layouts  104 us (20%)
  matrix products  57.9 us (11%)
  between operations  26 us (5%)
  starting transfers between devices  20.8 us (4%)
    psum x2, waiting for transfers between devices, on_device(): summed = lax.psum(lax.psum(local_term, 'dp'), ('ha', 'wa'))  171 us
    dot_general x6, matrix products, product(): jnp.einsum(pattern, first_op, second_op, preferred_element_type=jnp.float32)  45.4 us
    mul x1, local copies, waits for them, and re-layouts, query_back(): product('jhqk,jqhd->jkhd', score_grad, query_heads) * score_scale  25.5 us
    another operation x5, local copies, waits for them, and re-layouts  23.6 us
    another operation x2, other arithmetic, query_side(): return (query_grad, jnp.stack([key_part, value_part]))  21 us
    another operation x6, other arithmetic, spread_window(): return jnp.stack(spread_rows)  19 us
    add x1, other arithmetic, on_device(): padded_grad = placed if padded_grad is None else padded_grad + placed  18.3 us
    ppermute x2, waiting for transfers between devices, with_halo(): after = lax.ppermute(first, axis, down)  15.6 us
  transfers between devices with their start and end apart: 11, of which 5 were waited for; matrix products, arithmetic and copies ran while one was open for 26% of the time, Pallas kernels for 0%

profile of v1, /device:TPU:0, one launch (start us, length us, event | category | flops | bytes accessed | tf_op | source)
XLA Modules:
  0.0 513.1 jit_solution(16395398986275499475)
XLA Ops:
  10.5 5.6 %collective-permute-start = (bf16[2,1,1,1,384,512]{5,4,3,2,1,0:T(8,128)(2,1)S(1)}, bf16[2,1,1,1,384,512]{5,4,3,2,1,0:T(8,128)(2,1)S(1)}, u32[]{:S(2)}, u32[]{:S(2)}) collective-permute-start(bf16[2,1,1,1,384,512]{5,4,3,2,1,0:T(8,128)(2,1)S(1)} %pad_maximum_fusion.4), channel_id=1, source_target_pairs={{0,4},{4,8},{8,12},{1,5},{5,9},{9,13},{2,6},{6,10},{10,14},{3,7},{... | collective-permute-start | bytes 2359304 | tf_op jit(solution)/shard_map/ppermute | solution.py:27
  16.1 15.6 %collective-permute-done.1 = bf16[2,1,1,1,384,512]{5,4,3,2,1,0:T(8,128)(2,1)S(1)} collective-permute-done((bf16[2,1,1,1,384,512]{5,4,3,2,1,0:T(8,128)(2,1)S(1)}, bf16[2,1,1,1,384,512]{5,4,3,2,1,0:T(8,128)(2,1)S(1)}, u32[]{:S(2)}, u32[]{:S(2)}) %collective-permute-start.1) | collective-permute-done | bytes 786464 | tf_op jit(solution)/shard_map/ppermute | solution.py:28
  37.2 4.5 collective-permute-start.2
  63.6 3.8 pad_maximum_fusion
  71.4 7.2 %reshape.242 = bf16[3456,4,128]{2,1,0:T(4,128)(2,1)} reshape(bf16[1,9,384,512]{3,2,1,0:T(8,128)(2,1)} %pad_maximum_fusion.2) | data formatting | bytes 7077888 | tf_op jit(solution)/shard_map/reshape.31
  78.7 6.8 %copy.102 = bf16[3456,4,128]{0,2,1:T(8,128)(2,1)} copy(bf16[3456,4,128]{2,1,0:T(4,128)(2,1)} %reshape.242) | data formatting | bytes 7077888 | tf_op jit(solution)/shard_map/reshape.31
  85.5 7.5 %bitcast_reduce_fusion = (f32[4,384]{1,0:T(4,128)S(1)}, f32[4,3456,384]{2,1,0:T(8,128)S(1)}) fusion(pred[3456]{0:T(1024)(128)(4,1)S(1)} %broadcast_in_dim.69, bf16[3456,4,128]{0,2,1:T(8,128)(2,1)} %copy.102, bf16[384,4,128]{2,1,0:T(4,128)(2,1)S(1)} %copy-done.10), kind=kOutput, calls=%fused_computation.2 | convolution fusion | flops 1374878208 | bytes 25175424 | tf_op jit(solution)/shard_map/while/body/eval_jaxpr/jqhd,jkhd->jhqk/dot_general | solution.py:34
  93.0 5.7 %fusion.1 = f32[4,384]{1,0:T(4,128)S(1)} fusion(f32[4,3456,384]{2,1,0:T(8,128)S(1)} %get-tuple-element.125, f32[4,384]{1,0:T(4,128)S(1)} %get-tuple-element.124, pred[3456]{0:T(1024)(128)(4,1)S(1)} %broadcast_in_dim.69), kind=kLoop, calls=%fused_computation.4 | loop fusion | flops 21232128 | bytes 21249408 | tf_op jit(solution)/shard_map/while/body/eval_jaxpr/reduce_sum | solution.py:92
  98.7 7.4 %fusion.3 = bf16[4,384,3456]{1,2,0:T(8,128)(2,1)} fusion(f32[4,3456,384]{2,1,0:T(8,128)S(1)} %get-tuple-element.125, f32[4,384]{1,0:T(4,128)S(1)} %log_add_fusion, pred[3456]{0:T(1024)(128)(4,1)S(1)} %broadcast_in_dim.69), kind=kLoop, calls=%fused_computation.6 | loop fusion | flops 21233664 | bytes 31860096 | tf_op jit(solution)/shard_map/while/body/eval_jaxpr/convert_element_type | solution.py:93
  108.0 7.5 %reshape.241 = bf16[3456,4,128]{2,1,0:T(4,128)(2,1)} reshape(bf16[1,9,384,512]{3,2,1,0:T(8,128)(2,1)} %pad_maximum_fusion.1) | data formatting | bytes 7077888 | tf_op jit(solution)/shard_map/reshape.41
  115.5 10.3 %convolution_bitcast_fusion = f32[1,3456,4,128]{1,3,2,0:T(8,128)} fusion(bf16[384,4,128]{0,2,1:T(8,128)(2,1)S(1)} %bitcast.185, bf16[4,384,3456]{1,2,0:T(8,128)(2,1)} %fusion.3), kind=kOutput, calls=%fused_computation.15 | convolution fusion | flops 1358954496 | bytes 18087936 | tf_op jit(solution)/shard_map/while/body/eval_jaxpr/jhqk,jqhd->jkhd/dot_general | solution.py:34
  125.8 6.3 %multiply_reduce_fusion = (f32[384,4]{0,1:T(4,128)S(1)}, bf16[4,128,384]{2,1,0:T(8,128)(2,1)S(1)}) fusion(f32[1,384,4,128]{1,3,2,0:T(8,128)S(1)} %bitcast.195, bf16[4,384,3456]{1,2,0:T(8,128)(2,1)} %fusion.3, bf16[3456,4,128]{2,1,0:T(4,128)(2,1)S(1)} %copy-done.3), kind=kOutput, calls=%fused_computation.75 | convolution fusion | flops 1359739392 | bytes 15341568 | tf_op jit(solution)/shard_map/while/body/eval_jaxpr/jhqk,jkhd->jqhd/dot_general | solution.py:34
  132.1 12.1 %multiply_convert_fusion = bf16[4,384,3456]{1,2,0:T(8,128)(2,1)} fusion(bf16[4,384,3456]{1,2,0:T(8,128)(2,1)} %fusion.3, bf16[384,4,128]{0,2,1:T(8,128)(2,1)S(1)} %bitcast.186, f32[4,384]{1,0:T(4,128)S(1)} %bitcast.197, bf16[3456,4,128]{2,1,0:T(4,128)(2,1)} %reshape.241), kind=kOutput, calls=%fused_computation.7 | convolution fusion | flops 1380188160 | bytes 25171968 | tf_op jit(solution)/shard_map/while/body/eval_jaxpr/jqhd,jkhd->jhqk/dot_general | solution.py:34
  144.2 9.1 %copy.108 = f32[1,3456,4,128]{3,2,0,1:T(4,128)} copy(f32[1,3456,4,128]{1,3,2,0:T(8,128)} %convolution_bitcast_fusion) | data formatting | bytes 14155776 | tf_op jit(solution)/shard_map/while/body/eval_jaxpr/jhqk,jqhd->jkhd/transpose | solution.py:34
  153.3 8.3 %slice_bitcast_fusion.23 = (f32[1,384,512]{2,0,1:T(1,128)}, f32[1,384,512]{2,0,1:T(1,128)}, f32[1,384,512]{2,0,1:T(1,128)}, f32[1,384,512]{2,0,1:T(1,128)}, f32[...) fusion(f32[1,3,3,384,512]{4,0,3,2,1:T(1,128)} %bitcast.183), kind=kLoop, calls=%fused_computation.64 | loop fusion | bytes 14155776 | tf_op jit(solution)/shard_map/while/body/eval_jaxpr/squeeze | solution.py:64
  164.6 25.5 %copy.105 = f32[1,3456,4,128]{3,2,0,1:T(4,128)S(1)} copy(f32[1,3456,4,128]{3,1,2,0:T(8,128)S(1)} %multiply_bitcast_fusion) | data formatting | bytes 14155776 | tf_op jit(solution)/shard_map/while/body/eval_jaxpr/mul | solution.py:120
  190.2 4.2 slice_bitcast_fusion.32
  194.3 4.4 fusion.9
  210.0 10.9 %maximum_bitcast_fusion.2 = f32[1,3,3,384,512]{4,2,3,1,0:T(4,128)} fusion(f32[1,3,384,512]{3,1,2,0:T(4,128)} %add_bitcast_fusion, f32[1,3,384,512]{3,1,2,0:T(4,128)} %add_bitcast_fusion.1, f32[1,3,384,512]{3,1,2,0:T(4,128)} %add_bitcast_fusion.2), kind=kLoop, calls=%fused_computation.12 | loop fusion | flops 3538944 | bytes 14155776 | tf_op jit(solution)/shard_map/while/body/eval_jaxpr/stack | solution.py:198
  230.4 10.1 %maximum_bitcast_fusion.1 = f32[1,3,3,384,512]{4,2,3,1,0:T(4,128)} fusion(f32[1,3,384,512]{3,1,2,0:T(4,128)} %add_bitcast_fusion.3, f32[1,3,384,512]{3,1,2,0:T(4,128)} %add_bitcast_fusion.4, f32[1,3,384,512]{3,1,2,0:T(4,128)} %add_bitcast_fusion.5), kind=kLoop, calls=%fused_computation.11 | loop fusion | flops 3538944 | bytes 14155776 | tf_op jit(solution)/shard_map/while/body/eval_jaxpr/stack | solution.py:198
  240.5 10.7 %maximum_bitcast_fusion = f32[1,1,2,3,3,384,512]{6,4,5,3,2,1,0:T(4,128)S(1)} fusion(f32[1,3,3,384,512]{4,2,3,1,0:T(4,128)} %maximum_bitcast_fusion.2, f32[1,3,3,384,512]{4,2,3,1,0:T(4,128)} %maximum_bitcast_fusion.1), kind=kLoop, calls=%fused_computation.9 | loop fusion | flops 3538944 | bytes 28311552 | tf_op jit(solution)/shard_map/reshape | solution.py:203
  251.2 7.8 %slice_bitcast_fusion.2 = (f32[1,1,2,3,384,512]{5,3,4,2,1,0:T(4,128)}, f32[1,1,2,3,384,512]{5,3,4,2,1,0:T(4,128)}, f32[1,1,2,3,384,512]{5,3,4,2,1,0:T(4,128)}) fusion(f32[1,1,2,3,3,384,512]{6,4,5,3,2,1,0:T(4,128)S(1)} %maximum_bitcast_fusion), kind=kLoop, calls=%fused_computation.20 | loop fusion | bytes 28311552 | tf_op jit(solution)/shard_map/squeeze | solution.py:209
  259.0 18.3 %pad_add_fusion = (f32[1,3,2,3,384,512]{5,3,4,2,1,0:T(4,128)}, bf16[1,3,2,3,384,512]{5,3,4,2,1,0:T(4,128)(2,1)S(1)}) fusion(f32[1,1,2,3,384,512]{5,3,4,2,1,0:T(4,128)} %get-tuple-element.86, f32[1,1,2,3,384,512]{5,3,4,2,1,0:T(4,128)} %get-tuple-element.87, f32[1,1,2,3,384,512]{5,3,4,2,1,0:T(4,128)} %get-tuple-element.85), kind=kLoop, calls=%fused_computation.10 | loop fusion | flops 10616832 | bytes 35389440 | tf_op jit(solution)/shard_map/add | solution.py:212
  281.5 3.5 collective-permute-start.5
  288.3 71.1 %all-reduce.24.cloned.1.call-done = f32[512,3072]{1,0:T(8,128)} async-done(((f32[512,3072]{1,0:T(8,128)}), f32[512,3072]{1,0:T(8,128)}) %all-reduce.24.cloned.1.call-update) | async-done | bytes 6291472 | tf_op jit(solution)/shard_map/psum | solution.py:236
  359.4 12.9 %fusion.24 = (bf16[1,1,2,3,384,512]{5,3,4,2,1,0:T(4,128)(2,1)S(1)}, f32[1,1,2,3,384,512]{5,3,4,2,1,0:T(4,128)}) fusion(bf16[1,2,3,384,512]{4,3,2,1,0:T(8,128)(2,1)S(1)} %collective-permute-done.5, bf16[1,2,3,384,512]{4,3,2,1,0:T(8,128)(2,1)} %collective-permute-done.4, f32[1,3,2,3,384,512]{5,3,4,2,1,0:T(4,128)} %get-tuple-element.83), kind=kLoop, calls=%fused_computation.84 | loop fusion | flops 5898240 | bytes 16515072 | tf_op jit(solution)/shard_map/convert.6
  372.3 3.4 slice_bitcast_fusion.6
  378.9 6.3 %convolution_multiply_fusion = f32[4,128,384]{2,1,0:T(8,128)S(1)} fusion(bf16[3456,4,128]{0,2,1:T(8,128)(2,1)S(1)} %copy-done.4, bf16[4,384,3456]{1,2,0:T(8,128)(2,1)} %multiply_convert_fusion), kind=kOutput, calls=%fused_computation.45 | convolution fusion | flops 1359151104 | bytes 14942208 | tf_op jit(solution)/shard_map/while/body/eval_jaxpr/jhqk,jkhd->jqhd/dot_general | solution.py:34
  386.4 4.8 fusion.5
  392.4 7.1 %fusion.13 = f32[1,1,2,1,384,512]{5,3,4,2,1,0:T(1,128)S(1)} fusion(f32[1,1,2,3,384,512]{5,3,4,2,1,0:T(4,128)} %get-tuple-element.82, bf16[1,1,2,384,512]{4,0,3,2,1:T(2,128)(2,1)} %copy-done.33, bf16[1,1,2,384,512]{4,0,3,2,1:T(2,128)(2,1)} %collective-permute-done.6), kind=kLoop, calls=%fused_computation.44 | loop fusion | flops 1572864 | bytes 4718592 | tf_op jit(solution)/shard_map/add | solution.py:225
  402.4 99.8 %all-reduce.26.cloned.1.call-done = f32[512,3072]{1,0:T(8,128)} async-done(((f32[512,3072]{1,0:T(8,128)}), f32[512,3072]{1,0:T(8,128)}) %all-reduce.26.cloned.1.call-update) | async-done | bytes 6291472 | tf_op jit(solution)/shard_map/psum | solution.py:236
  502.2 3.9 constant_dynamic-slice_fusion
  (119 shorter events, 64.9 us)
Async XLA Ops:
  7.2 50.0 %copy-start = (bf16[1,1,1,384,3072]{4,3,2,1,0:T(8,128)(2,1)S(1)}, bf16[1,1,1,384,3072]{4,3,2,1,0:T(8,128)(2,1)}, u32[]{:S(2)}) copy-start(bf16[1,1,1,384,3072]{4,3,2,1,0:T(8,128)(2,1)} %param.8) | copy-start | bytes 7077892
  7.2 50.0 %all-gather.2.cloned.1.call-start = ((), (), s32[]{:S(2)}) async-start(), calls=%async_computation | async-start | bytes 4718592 | tf_op jit(solution)/shard_map/all_gather | solution.py:154
  7.9 46.1 %copy-start.34 = (bf16[1,1,1,384,512]{4,3,2,1,0:T(8,128)(2,1)S(1)}, bf16[1,1,1,384,512]{4,3,2,1,0:T(8,128)(2,1)}, u32[]{:S(2)}) copy-start(bf16[1,1,1,384,512]{4,3,2,1,0:T(8,128)(2,1)} %param.5) | copy-start | bytes 1179652
  7.9 351.4 %all-reduce.24.cloned.1.call-start = ((), (), s32[]{:S(2)}) async-start(), calls=%async_computation.1 | async-start | bytes 12582912 | tf_op jit(solution)/shard_map/psum | solution.py:236
  9.2 22.5 %collective-permute-start.1 = (bf16[2,1,1,1,384,512]{5,4,3,2,1,0:T(8,128)(2,1)S(1)}, bf16[2,1,1,1,384,512]{5,4,3,2,1,0:T(8,128)(2,1)S(1)}, u32[]{:S(2)}, u32[]{:S(2)}) collective-permute-start(bf16[2,1,1,1,384,512]{5,4,3,2,1,0:T(8,128)(2,1)S(1)} %pad_maximum_fusion.4), channel_id=1, source_target_pairs={{4,0},{8,4},{12,8},{5,1},{9,5},{13,9},{6,2},{10,6},{14,10},{7,3},{... | collective-permute-start | bytes 2359304 | tf_op jit(solution)/shard_map/ppermute | solution.py:28
  10.5 22.4 %collective-permute-start = (bf16[2,1,1,1,384,512]{5,4,3,2,1,0:T(8,128)(2,1)S(1)}, bf16[2,1,1,1,384,512]{5,4,3,2,1,0:T(8,128)(2,1)S(1)}, u32[]{:S(2)}, u32[]{:S(2)}) collective-permute-start(bf16[2,1,1,1,384,512]{5,4,3,2,1,0:T(8,128)(2,1)S(1)} %pad_maximum_fusion.4), channel_id=1, source_target_pairs={{0,4},{4,8},{8,12},{1,5},{5,9},{9,13},{2,6},{6,10},{10,14},{3,7},{... | collective-permute-start | bytes 2359304 | tf_op jit(solution)/shard_map/ppermute | solution.py:27
  36.0 27.6 %collective-permute-start.3 = (bf16[2,1,3,1,384,512]{5,4,3,2,1,0:T(8,128)(2,1)}, bf16[2,1,3,1,384,512]{5,4,3,2,1,0:T(8,128)(2,1)}, u32[]{:S(2)}, u32[]{:S(2)}) collective-permute-start(bf16[2,1,3,1,384,512]{5,4,3,2,1,0:T(8,128)(2,1)} %pad_maximum_fusion.3), channel_id=1, source_target_pairs={{1,0},{2,1},{3,2},{5,4},{6,5},{7,6},{9,8},{10,9},{11,10},{13,12},{... | collective-permute-start | bytes 7077896 | tf_op jit(solution)/shard_map/ppermute | solution.py:28
  37.2 26.3 %collective-permute-start.2 = (bf16[2,1,3,1,384,512]{5,4,3,2,1,0:T(8,128)(2,1)}, bf16[2,1,3,1,384,512]{5,4,3,2,1,0:T(8,128)(2,1)}, u32[]{:S(2)}, u32[]{:S(2)}) collective-permute-start(bf16[2,1,3,1,384,512]{5,4,3,2,1,0:T(8,128)(2,1)} %pad_maximum_fusion.3), channel_id=1, source_target_pairs={{0,1},{1,2},{2,3},{4,5},{5,6},{6,7},{8,9},{9,10},{10,11},{12,13},{... | collective-permute-start | bytes 7077896 | tf_op jit(solution)/shard_map/ppermute | solution.py:27
  54.9 8.7 %copy-start.8 = (bf16[1,1,1,384,512]{4,3,2,1,0:T(8,128)(2,1)S(1)}, bf16[1,1,1,384,512]{4,3,2,1,0:T(8,128)(2,1)}, u32[]{:S(2)}) copy-start(bf16[1,1,1,384,512]{4,3,2,1,0:T(8,128)(2,1)} %param.7) | copy-start | bytes 1179652
  54.9 8.7 %copy-start.9 = (bf16[1,1,1,384,512]{4,3,2,1,0:T(8,128)(2,1)S(1)}, bf16[1,1,1,384,512]{4,3,2,1,0:T(8,128)(2,1)}, u32[]{:S(2)}) copy-start(bf16[1,1,1,384,512]{4,3,2,1,0:T(8,128)(2,1)} %param.6) | copy-start | bytes 1179652
  78.7 6.8 %copy-start.10 = (bf16[384,4,128]{2,1,0:T(4,128)(2,1)S(1)}, bf16[384,4,128]{2,1,0:T(4,128)(2,1)}, u32[]{:S(2)}) copy-start(bf16[384,4,128]{2,1,0:T(4,128)(2,1)} %reshape.243) | copy-start | bytes 1179652
  98.7 7.4 %copy-start.5 = (bf16[1,3,384,512]{3,2,1,0:T(8,128)(2,1)S(1)}, bf16[1,3,384,512]{3,2,1,0:T(8,128)(2,1)}, u32[]{:S(2)}) copy-start(bf16[1,3,384,512]{3,2,1,0:T(8,128)(2,1)} %get-tuple-element.108) | copy-start | bytes 3538948
  98.7 7.4 %copy-start.6 = (bf16[1,3,384,512]{3,2,1,0:T(8,128)(2,1)S(1)}, bf16[1,3,384,512]{3,2,1,0:T(8,128)(2,1)}, u32[]{:S(2)}) copy-start(bf16[1,3,384,512]{3,2,1,0:T(8,128)(2,1)} %get-tuple-element.112) | copy-start | bytes 3538948
  98.7 7.4 %copy-start.7 = (bf16[1,3,384,512]{3,2,1,0:T(8,128)(2,1)S(1)}, bf16[1,3,384,512]{3,2,1,0:T(8,128)(2,1)}, u32[]{:S(2)}) copy-start(bf16[1,3,384,512]{3,2,1,0:T(8,128)(2,1)} %get-tuple-element.113) | copy-start | bytes 3538948
  115.5 10.3 %copy-start.3 = (bf16[3456,4,128]{2,1,0:T(4,128)(2,1)S(1)}, bf16[3456,4,128]{2,1,0:T(4,128)(2,1)}, u32[]{:S(2)}) copy-start(bf16[3456,4,128]{2,1,0:T(4,128)(2,1)} %reshape.241) | copy-start | bytes 10616836
  115.5 10.3 %copy-start.11 = (f32[384,512]{0,1:T(8,128)S(1)}, f32[384,512]{0,1:T(8,128)}, u32[]{:S(2)}) copy-start(f32[384,512]{0,1:T(8,128)} %copy.100) | copy-start | bytes 2359300
  153.3 8.3 %copy-start.2 = (bf16[4,384,3456]{1,2,0:T(8,128)(2,1)S(1)}, bf16[4,384,3456]{1,2,0:T(8,128)(2,1)}, u32[]{:S(2)}) copy-start(bf16[4,384,3456]{1,2,0:T(8,128)(2,1)} %multiply_convert_fusion) | copy-start | bytes 31850500
  198.8 303.5 %all-reduce.26.cloned.1.call-start = ((), (), s32[]{:S(2)}) async-start(), calls=%async_computation.2 | async-start | bytes 12582912 | tf_op jit(solution)/shard_map/psum | solution.py:236
  198.8 4.7 copy-start.26
  198.9 4.7 copy-start.27
  198.9 4.7 copy-start.28
  203.5 3.3 copy-start.21
  203.5 3.3 copy-start.22
  210.0 10.9 %copy-start.23 = (f32[1,384,512]{2,0,1:T(1,128)S(1)}, f32[1,384,512]{2,0,1:T(1,128)}, u32[]{:S(2)}) copy-start(f32[1,384,512]{2,0,1:T(1,128)} %get-tuple-element.91) | copy-start | bytes 2359300
  210.0 10.9 %copy-start.24 = (f32[1,384,512]{2,0,1:T(1,128)S(1)}, f32[1,384,512]{2,0,1:T(1,128)}, u32[]{:S(2)}) copy-start(f32[1,384,512]{2,0,1:T(1,128)} %get-tuple-element.92) | copy-start | bytes 2359300
  210.0 10.9 %copy-start.25 = (f32[1,384,512]{2,0,1:T(1,128)S(1)}, f32[1,384,512]{2,0,1:T(1,128)}, u32[]{:S(2)}) copy-start(f32[1,384,512]{2,0,1:T(1,128)} %get-tuple-element.93) | copy-start | bytes 2359300
  281.5 77.9 %collective-permute-start.5 = (bf16[1,2,3,384,512]{4,3,2,1,0:T(8,128)(2,1)}, bf16[1,2,3,384,512]{4,3,2,1,0:T(8,128)(2,1)S(1)}, u32[]{:S(2)}, u32[]{:S(2)}) collective-permute-start(bf16[1,2,3,384,512]{4,3,2,1,0:T(8,128)(2,1)} %copy.113), channel_id=1, source_target_pairs={{0,4},{4,8},{8,12},{1,5},{5,9},{9,13},{2,6},{6,10},{10,14},{3,7},{... | collective-permute-start | bytes 7077896 | tf_op jit(solution)/shard_map/ppermute | solution.py:17
  287.0 72.4 %collective-permute-start.4 = (bf16[1,2,3,384,512]{4,3,2,1,0:T(8,128)(2,1)}, bf16[1,2,3,384,512]{4,3,2,1,0:T(8,128)(2,1)}, u32[]{:S(2)}, u32[]{:S(2)}) collective-permute-start(bf16[1,2,3,384,512]{4,3,2,1,0:T(8,128)(2,1)} %copy.111), channel_id=1, source_target_pairs={{4,0},{8,4},{12,8},{5,1},{9,5},{13,9},{6,2},{10,6},{14,10},{7,3},{... | collective-permute-start | bytes 7077896 | tf_op jit(solution)/shard_map/ppermute | solution.py:17
  372.3 6.6 %copy-start.4 = (bf16[3456,4,128]{0,2,1:T(8,128)(2,1)S(1)}, bf16[3456,4,128]{0,2,1:T(8,128)(2,1)}, u32[]{:S(2)}) copy-start(bf16[3456,4,128]{0,2,1:T(8,128)(2,1)} %copy.102) | copy-start | bytes 10616836
  375.7 15.5 %collective-permute-start.7 = (bf16[1,1,2,384,512]{4,0,3,2,1:T(2,128)(2,1)}, bf16[1,1,2,384,512]{4,0,3,2,1:T(2,128)(2,1)S(1)}, u32[]{:S(2)}, u32[]{:S(2)}) collective-permute-start(bf16[1,1,2,384,512]{4,0,3,2,1:T(2,128)(2,1)} %get-tuple-element.115), channel_id=1, source_target_pairs={{0,1},{1,2},{2,3},{4,5},{5,6},{6,7},{8,9},{9,10},{10,11},{12,13},{... | collective-permute-start | bytes 2359304 | tf_op jit(solution)/shard_map/ppermute | solution.py:17
  377.4 13.8 %collective-permute-start.6 = (bf16[1,1,2,384,512]{4,0,3,2,1:T(2,128)(2,1)}, bf16[1,1,2,384,512]{4,0,3,2,1:T(2,128)(2,1)}, u32[]{:S(2)}, u32[]{:S(2)}) collective-permute-start(bf16[1,1,2,384,512]{4,0,3,2,1:T(2,128)(2,1)} %get-tuple-element.114), channel_id=1, source_target_pairs={{1,0},{2,1},{3,2},{5,4},{6,5},{7,6},{9,8},{10,9},{11,10},{13,12},{... | collective-permute-start | bytes 2359304 | tf_op jit(solution)/shard_map/ppermute | solution.py:17
  401.5 104.7 %copy-start.1 = (bf16[1,1,1,384,3072]{4,3,2,1,0:T(8,128)(2,1)S(1)}, bf16[1,1,1,384,3072]{4,3,2,1,0:T(8,128)(2,1)}, u32[]{:S(2)}) copy-start(bf16[1,1,1,384,3072]{4,3,2,1,0:T(8,128)(2,1)} %param.8) | copy-start | bytes 7077892
  (14 other events, 32.7 us)
Sparse Core Ops, SparseCore 0:
  9.5 47.6 all-gather.1
  198.9 160.3 all-reduce.23
  363.0 139.2 all-reduce.25
